TPU v7x, 32 devices: a whole 2x2x4 slice. The times are simulated.
32 devices in a mesh: pair: 4 (over y, core), fold: 8 (over z, x).
Axes of the slice: x: 2, y: 2, z: 4, core: 2. Of those that a mesh axis runs over, the one named last changes fastest.
Arguments:
- amplitudes: bfloat16 [4, 80, 640, 640], P(None, 'pair', 'fold'), may hold values from -6 to 6
- cycle_block: bfloat16 [640, 80, 8, 640], P('fold', None, 'pair'), may hold values from -0.078125 to 0.078125
- occ_sizes: int32 [8], replicated, may hold values from 1 to 20, 80 in all
- vir_sizes: int32 [8], replicated, may hold values from 1 to 160, 640 in all
- window_i: int32 [4], replicated, may hold values from 0 to 79
- window_occ: int32 [8], replicated, may hold values from 0 to 79
Outputs:
- residual: bfloat16 [4, 640, 8, 640], P(None, 'fold', 'pair')
Inputs may be any that keep to these rules, and one draw needn't show every extreme that they name: `occ_sizes`: the entries sum to 80. `vir_sizes`: the entries sum to 640.
All inputs are finite; a program needn't handle non-finite values.
Results may differ from a plain program's by a relative error of at most 0.001.
Values may be sent and summed in bfloat16 or wider, within the bound.
A program may use at most 128 MiB of HBM per device.

v0:
```python
import jax
import jax.numpy as jnp
from jax import lax
from jax.sharding import PartitionSpec as P

FOLDS = 4


def irrep_labels(sizes, count):
    boundaries = jnp.cumsum(sizes)
    positions = jnp.arange(count, dtype=jnp.int32)
    return jnp.sum((positions[:, None] >= boundaries[None, :]).astype(jnp.int32), axis=1)


def label_lookup(orbitals, labels, count):
    matches = orbitals[:, None] == jnp.arange(count, dtype=jnp.int32)[None, :]
    return jnp.sum(jnp.where(matches, labels[None, :], 0), axis=1)


def body(n_pair, n_fold, amplitudes, cycle_block, occ_sizes, vir_sizes, window_i, window_occ):
    c_local, occ_total, j_local, vir_total = cycle_block.shape
    n_i, k_local, a_rows, _ = amplitudes.shape
    v_pack = vir_total // FOLDS
    k_pack = occ_total // FOLDS
    a_sub = a_rows // n_pair
    fold = lax.axis_index("fold")
    pair = lax.axis_index("pair")
    occ_labels = irrep_labels(occ_sizes, occ_total)
    vir_labels = irrep_labels(vir_sizes, vir_total)
    c_labels = lax.dynamic_slice_in_dim(vir_labels, fold * c_local, c_local)
    a_labels = lax.dynamic_slice_in_dim(vir_labels, fold * a_rows, a_rows)
    k_labels = lax.dynamic_slice_in_dim(occ_labels, pair * k_local, k_local)
    i_labels = label_lookup(window_i, occ_labels, occ_total)
    j_orbitals = lax.dynamic_slice_in_dim(window_occ, pair * j_local, j_local)
    j_labels = label_lookup(j_orbitals, occ_labels, occ_total)
    ika = i_labels[:, None, None] ^ k_labels[None, :, None] ^ a_labels[None, None, :]
    packed_c = 0
    for q in range(FOLDS):
        cut = slice(q * v_pack, (q + 1) * v_pack)
        keep = ika[..., None] == vir_labels[cut]
        packed_c = packed_c + jnp.where(keep, amplitudes[..., cut], 0)
    moved = lax.all_to_all(
        packed_c.reshape(n_i, k_local, n_pair, a_sub, v_pack),
        "pair",
        split_axis=2,
        concat_axis=1,
        tiled=True,
    ).reshape(n_i, FOLDS, k_pack, a_sub, v_pack)
    own_a = lax.dynamic_slice_in_dim(a_labels, pair * a_sub, a_sub)
    ia = i_labels[:, None] ^ own_a[None, :]
    pieces = []
    for q in range(FOLDS):
        iac = ia[..., None] ^ vir_labels[q * v_pack : (q + 1) * v_pack]
        total = 0
        for s in range(FOLDS):
            keep = iac[:, None] == occ_labels[s * k_pack : (s + 1) * k_pack][None, :, None, None]
            total = total + jnp.where(keep, moved[:, s], 0)
        pieces.append(total)
    packed_k = jnp.concatenate(pieces, axis=-1)
    packed_k = packed_k.reshape(n_i, k_pack, a_sub, n_fold, c_local).transpose(3, 0, 2, 1, 4)
    packed_k = packed_k.reshape(n_fold, n_i * a_sub, k_pack * c_local)
    relaid = lax.all_to_all(packed_k, "fold", split_axis=0, concat_axis=0, tiled=True)
    gathered = lax.all_gather(relaid, "pair", axis=0, tiled=False)
    ckj = c_labels[:, None, None] ^ occ_labels[None, :, None] ^ j_labels[None, None, :]
    packed_w = 0
    for q in range(FOLDS):
        cut = slice(q * v_pack, (q + 1) * v_pack)
        keep = ckj[..., None] == vir_labels[cut]
        packed_w = packed_w + jnp.where(keep, cycle_block[..., cut], 0)
    packed_w = packed_w.reshape(c_local, FOLDS, k_pack, j_local * v_pack).transpose(1, 2, 0, 3)
    packed_w = packed_w.reshape(FOLDS, k_pack * c_local, j_local * v_pack)
    row_a = vir_labels.reshape(n_fold, n_pair, a_sub).transpose(1, 0, 2)
    row_labels = (row_a[:, :, None, :] ^ i_labels[:, None]).reshape(n_pair, n_fold, n_i * a_sub)
    partial_sum = 0
    for s in range(FOLDS):
        col_labels = (
            occ_labels[s * k_pack : (s + 1) * k_pack][:, None] ^ c_labels[None, :]
        ).reshape(-1)
        lhs = jnp.where(row_labels[..., None] == col_labels, gathered, 0)
        partial_sum = partial_sum + jnp.einsum(
            "pfrx,xn->fprn", lhs, packed_w[s], preferred_element_type=jnp.float32
        )
    flat = partial_sum.reshape(-1, j_local * v_pack)
    own = lax.psum_scatter(flat, "fold", scatter_dimension=0, tiled=True)
    own = own.astype(jnp.bfloat16).reshape(n_pair, n_i, a_sub, j_local, v_pack)
    own = own.transpose(1, 0, 2, 3, 4).reshape(n_i, a_rows, j_local, v_pack)
    iaj = i_labels[:, None, None] ^ a_labels[None, :, None] ^ j_labels[None, None, :]
    keep = iaj[..., None] == vir_labels
    return jnp.where(keep, jnp.concatenate([own] * FOLDS, axis=-1), 0)


def solution(mesh):
    sizes = (mesh.shape["pair"], mesh.shape["fold"])
    placed = (P(None, "pair", "fold", None), P("fold", None, "pair", None), P(), P(), P(), P())

    def run(*args):
        return body(*sizes, *args)

    return jax.shard_map(
        run, mesh=mesh, in_specs=placed, out_specs=P(None, "fold", "pair", None), check_vma=False
    )
```

profile of v0, /device:TPU:0, one launch (start us, length us, event | category | flops | bytes accessed | tf_op | source)
XLA Modules:
  0.0 380.5 jit_solution(2479154911337334194)
XLA Ops:
  6.5 0.8 reduce-window.17
  7.7 0.8 reduce-window.16
  9.3 0.8 select_reduce_fusion
  10.2 9.5 %fusion.21 = bf16[4,20,80,160]{3,2,1,0:T(8,128)(2,1)S(1)} fusion(bf16[4,20,80,640]{3,2,1,0:T(8,128)(2,1)} %param.6, s32[160]{0:T(256)S(1)} %get-tuple-element.22, s32[160]{0:T(256)S(1)} %get-tuple-element.23, s32[160]{0:T(256)S(1)} %get-tuple-element.24, s32[160]{0:T(256)S(1)} %get-tuple-element.21, s32[4,20,80]{2,1,0:T(8,128)S(1)} %broadcast_xor_fusion.6), kind=kLoop, calls=%fused_computation.35 | loop fusion | flops 11264000 | bytes 10268160 | tf_op jit(solution)/shard_map/add | solution.py:41
  19.8 2.5 copy.45
  22.3 2.9 copy.46
  25.2 4.3 %all-to-all-start = ((bf16[4,20,4,20,160]{4,0,3,1,2:T(4,128)(2,1)}), bf16[4,20,4,20,160]{4,0,3,1,2:T(4,128)(2,1)S(1)}, u32[]{:S(2)}, u32[]{:S(2)}) async-start(bf16[4,20,4,20,160]{4,0,3,1,2:T(4,128)(2,1)} %copy.46), calls=%async_computation | async-start | bytes 6553600 | tf_op jit(solution)/shard_map/all_to_all | solution.py:42
  32.0 1.5 broadcast_xor_fusion.5
  33.5 34.4 %all-to-all-done = bf16[4,20,4,20,160]{4,0,3,1,2:T(4,128)(2,1)S(1)} async-done(((bf16[4,20,4,20,160]{4,0,3,1,2:T(4,128)(2,1)}), bf16[4,20,4,20,160]{4,0,3,1,2:T(4,128)(2,1)S(1)}, u32[]{:S(2)}, u32[]{:S(2)}) %all-to-all-start) | async-done | bytes 2048032 | tf_op jit(solution)/shard_map/all_to_all | solution.py:42
  67.9 2.6 fusion.40
  70.5 3.0 squeeze.17
  73.5 2.5 squeeze.18
  76.0 2.5 squeeze.19
  78.5 2.5 squeeze.40
  81.0 16.6 %fusion.24 = (bf16[4,20,20,2,80]{4,3,0,2,1:T(2,128)(2,1)S(1)}, bf16[4,20,20,2,80]{4,3,0,2,1:T(2,128)(2,1)S(1)}, bf16[4,20,20,2,80]{4,3,0,2,1:T(2,128)(2,1)S(1)}, bf16[4,20,20,2,80]{4,3,0,2,1:T(2,128)(2,1)S(1)}) fusion(bf16[4,20,20,2,80]{4,3,0,2,1:T(2,128)(2,1)S(1)} %squeeze.40, s32[4,20,2,80]{3,2,0,1:T(2,128)S(1)} %get-tuple-element.17, ...), kind=kLoop, calls=%fused_computation.57 | loop fusion | flops 11264000 | bytes 4301120 | tf_op jit(solution)/shard_map/add | solution.py:57
  97.6 4.9 %maximum_bitcast_fusion = bf16[8,4,20,20,80]{4,0,1,2,3:T(8,128)(2,1)S(1)} fusion(bf16[4,20,20,2,80]{4,3,0,2,1:T(2,128)(2,1)S(1)} %get-tuple-element.10, bf16[4,20,20,2,80]{4,3,0,2,1:T(2,128)(2,1)S(1)} %get-tuple-element.11, bf16[4,20,20,2,80]{4,3,0,2,1:T(2,128)(2,1)S(1)} %get-tuple-element.12, bf16[4,20,20,2,80]{4,3,0,2,1:T(2,128)(2,1)S(1)} %get-tuple-element.9), kind=kLoop, calls=%fused_computation.36 | loop fusion | flops 8192000 | bytes 4096000 | tf_op jit(solution)/shard_map/transpose | solution.py:60
  102.5 4.1 %copy.47 = bf16[8,4,20,20,80]{4,3,2,1,0:T(8,128)(2,1)} copy(bf16[8,4,20,20,80]{4,0,1,2,3:T(8,128)(2,1)S(1)} %maximum_bitcast_fusion) | data formatting | bytes 4096000 | tf_op jit(solution)/shard_map/transpose | solution.py:60
  106.6 5.3 %reshape.385 = bf16[8,80,1600]{2,1,0:T(8,128)(2,1)S(1)} reshape(bf16[8,4,20,20,80]{4,3,2,1,0:T(8,128)(2,1)} %copy.47) | data formatting | bytes 4096000 | tf_op jit(solution)/shard_map/reshape | solution.py:61
  111.9 55.9 %all_to_all.20 = bf16[8,80,1600]{2,1,0:T(8,128)(2,1)} all-to-all(bf16[8,80,1600]{2,1,0:T(8,128)(2,1)S(1)} %reshape.385), channel_id=1, replica_groups=mesh['pair'=4,'fold'=8] {'fold'}, dimensions={0} | all-to-all | bytes 4096000 | tf_op jit(solution)/shard_map/all_to_all | solution.py:62
  168.5 0.9 broadcast_xor_fusion
  169.5 56.1 %fusion.14 = bf16[80,80,2,160]{3,2,1,0:T(2,128)(2,1)} fusion(bf16[80,80,2,640]{3,2,1,0:T(2,128)(2,1)} %param.7, s32[160]{0:T(256)S(1)} %get-tuple-element.22, s32[80,80,2]{2,1,0:T(8,128)S(1)} %broadcast_xor_fusion, s32[160]{0:T(256)S(1)} %get-tuple-element.23, s32[160]{0:T(256)S(1)} %copy-done.2, s32[160]{0:T(256)S(1)} %get-tuple-element.21), kind=kLoop, calls=%fused_computation.22 | loop fusion | flops 22528000 | bytes 20533760 | tf_op jit(solution)/shard_map/add | solution.py:69
  225.6 15.1 %reshape.394 = bf16[80,4,20,320]{3,2,1,0:T(8,128)(2,1)} reshape(bf16[80,80,2,160]{3,2,1,0:T(2,128)(2,1)} %fusion.14) | data formatting | bytes 8192000 | tf_op jit(solution)/shard_map/reshape | solution.py:70
  240.7 6.7 %copy.64 = bf16[80,4,20,320]{3,0,2,1:T(8,128)(2,1)} copy(bf16[80,4,20,320]{3,2,1,0:T(8,128)(2,1)} %reshape.394) | data formatting | bytes 8192000 | tf_op jit(solution)/shard_map/reshape | solution.py:70
  248.0 4.3 %fusion.39 = (bf16[1,20,80,320]{3,2,1,0:T(8,128)(2,1)S(1)}, bf16[1,20,80,320]{3,2,1,0:T(8,128)(2,1)S(1)}, bf16[1,20,80,320]{3,2,1,0:T(8,128)(2,1)}, bf16[1,20,80,320]{3,2,1,0:T(8,128)(2,1)}) fusion(bf16[4,20,80,320]{3,2,1,0:T(8,128)(2,1)} %bitcast.46), kind=kLoop, calls=%fused_computation.94 | loop fusion | bytes 8192000 | tf_op jit(solution)/shard_map/slice | solution.py:81
  252.3 8.1 %fusion.1 = f32[320,4,8,80]{0,3,2,1:T(8,128)S(1)} fusion(bf16[1600,320,1,1]{1,0,3,2:T(8,128)(2,1)} %bitcast.55, bf16[4,8,80,1600]{3,2,1,0:T(8,128)(2,1)} %bitcast.58, s32[1600]{0:T(1024)S(1)} %xor.329, s32[4,8,80]{2,1,0:T(8,128)S(1)} %broadcast_xor_fusion.8), kind=kOutput, calls=%fused_computation.9 | convolution fusion | flops 2629632000 | bytes 12509440 | tf_op jit(solution)/shard_map/pfrx,xn->fprn/dot_general | solution.py:80
  260.4 7.1 %fusion = f32[320,4,8,80]{0,3,2,1:T(8,128)} fusion(bf16[1600,320,1,1]{1,0,3,2:T(8,128)(2,1)S(1)} %bitcast.54, bf16[4,8,80,1600]{3,2,1,0:T(8,128)(2,1)S(1)} %bitcast.59, s32[1600]{0:T(1024)S(1)} %xor.306, s32[4,8,80]{2,1,0:T(8,128)S(1)} %broadcast_xor_fusion.8), kind=kOutput, calls=%fused_computation.8 | convolution fusion | flops 2629632000 | bytes 12509440 | tf_op jit(solution)/shard_map/pfrx,xn->fprn/dot_general | solution.py:80
  267.6 7.0 %fusion.2 = f32[320,4,8,80]{0,3,2,1:T(8,128)} fusion(bf16[1600,320,1,1]{1,0,3,2:T(8,128)(2,1)S(1)} %bitcast.53, bf16[4,8,80,1600]{3,2,1,0:T(8,128)(2,1)S(1)} %bitcast.60, s32[1600]{0:T(1024)S(1)} %xor.332, s32[4,8,80]{2,1,0:T(8,128)S(1)} %broadcast_xor_fusion.8), kind=kOutput, calls=%fused_computation.10 | convolution fusion | flops 2629632000 | bytes 12509440 | tf_op jit(solution)/shard_map/pfrx,xn->fprn/dot_general | solution.py:80
  274.6 8.2 %add_bitcast_fusion = f32[8,4,80,320]{3,2,0,1:T(8,128)S(1)} fusion(f32[320,4,8,80]{0,3,2,1:T(8,128)} %fusion.2, f32[320,4,8,80]{0,3,2,1:T(8,128)} %fusion, f32[320,4,8,80]{0,3,2,1:T(8,128)S(1)} %fusion.1, bf16[1600,320,1,1]{1,0,3,2:T(8,128)(2,1)S(1)} %bitcast.52, bf16[4,8,80,1600]{3,2,1,0:T(8,128)(2,1)S(1)} %bitcast.61, s32[1600]{0:T(1024)S(1)} %xor.335, ...), kind=kOutput, calls=%fused_computation.32 | convolution fusion | flops 2632089600 | bytes 22339840 | tf_op jit(solution)/shard_map/pfrx,xn->fprn/dot_general | solution.py:80
  282.9 2.2 copy.52
  285.3 82.2 %reduce-scatter.2.cloned.1.call-done = f32[320,320]{1,0:T(8,128)} async-done(((f32[2560,320]{1,0:T(8,128)}), f32[320,320]{1,0:T(8,128)}) %reduce-scatter.2.cloned.1.call-update) | async-done | bytes 409616 | tf_op jit(solution)/shard_map/reduce_scatter | solution.py:84
  367.5 1.1 convert_element_type.45
  369.0 4.5 %compare_select_fusion.32 = bf16[4,80,2,640]{3,2,1,0:T(2,128)(2,1)} fusion(bf16[4,80,2,160]{3,2,1,0:T(2,128)(2,1)S(1)} %bitcast.50, s32[640]{0:T(1024)S(1)} %convert_reduce_fusion, s32[4,80,2]{2,1,0:T(8,128)S(1)} %broadcast_xor_fusion.1), kind=kLoop, calls=%fused_computation.53 | loop fusion | flops 4096000 | bytes 1029120 | tf_op jit(solution)/shard_map/jit(_where)/select_n | solution.py:89
  (67 shorter events, 5.5 us)
Async XLA Ops:
  7.5 22.6 %copy-start.1 = (s32[160]{0:T(256)}, s32[160]{0:T(256)S(1)}, u32[]{:S(2)}) copy-start(s32[160]{0:T(256)S(1)} %get-tuple-element.24) | copy-start | bytes 1924
  7.6 12.2 %copy-start.3 = (s32[80]{0:T(128)}, s32[80]{0:T(128)S(1)}, u32[]{:S(2)}) copy-start(s32[80]{0:T(128)S(1)} %dynamic_slice.15) | copy-start | bytes 964
  10.1 9.7 %copy-start.11 = (s32[4]{0:T(128)}, s32[4]{0:T(128)S(1)}, u32[]{:S(2)}) copy-start(s32[4]{0:T(128)S(1)} %select_reduce_fusion) | copy-start | bytes 52
  25.2 42.7 %all-to-all-start = ((bf16[4,20,4,20,160]{4,0,3,1,2:T(4,128)(2,1)}), bf16[4,20,4,20,160]{4,0,3,1,2:T(4,128)(2,1)S(1)}, u32[]{:S(2)}, u32[]{:S(2)}) async-start(bf16[4,20,4,20,160]{4,0,3,1,2:T(4,128)(2,1)} %copy.46), calls=%async_computation | async-start | bytes 6553600 | tf_op jit(solution)/shard_map/all_to_all | solution.py:42
  29.5 222.8 %all-gather.3.cloned.1.call-start = ((), (), s32[]{:S(2)}) async-start(), calls=%async_computation.4 | async-start | bytes 10649600 | tf_op jit(solution)/shard_map/all_gather | solution.py:63
  70.5 10.5 %copy-start.5 = (s32[20]{0:T(128)S(1)}, s32[20]{0:T(128)}, u32[]{:S(2)}) copy-start(s32[20]{0:T(128)} %get-tuple-element.29) | copy-start | bytes 244
  70.5 10.5 %copy-start.6 = (s32[20]{0:T(128)S(1)}, s32[20]{0:T(128)}, u32[]{:S(2)}) copy-start(s32[20]{0:T(128)} %get-tuple-element.30) | copy-start | bytes 244
  70.5 10.5 %copy-start.8 = (s32[20]{0:T(128)S(1)}, s32[20]{0:T(128)}, u32[]{:S(2)}) copy-start(s32[20]{0:T(128)} %get-tuple-element.31) | copy-start | bytes 244
  111.8 56.1 %copy-start.4 = (s32[80]{0:T(128)S(1)}, s32[80]{0:T(128)}, u32[]{:S(2)}) copy-start(s32[80]{0:T(128)} %copy-done.3) | copy-start | bytes 964
  111.9 56.1 %copy-start.7 = (s32[20]{0:T(128)S(1)}, s32[20]{0:T(128)}, u32[]{:S(2)}) copy-start(s32[20]{0:T(128)} %get-tuple-element.30) | copy-start | bytes 244
  111.9 56.1 %copy-start.9 = (s32[20]{0:T(128)S(1)}, s32[20]{0:T(128)}, u32[]{:S(2)}) copy-start(s32[20]{0:T(128)} %get-tuple-element.31) | copy-start | bytes 244
  111.9 56.1 %copy-start.10 = (s32[20]{0:T(128)S(1)}, s32[20]{0:T(128)}, u32[]{:S(2)}) copy-start(s32[20]{0:T(128)} %get-tuple-element.32) | copy-start | bytes 244
  111.9 56.3 %copy-start.14 = (s32[8]{0:T(128)S(1)}, s32[8]{0:T(128)}, u32[]{:S(2)}) copy-start(s32[8]{0:T(128)} %param.11) | copy-start | bytes 100
  111.9 57.6 %copy-start.2 = (s32[160]{0:T(256)S(1)}, s32[160]{0:T(256)}, u32[]{:S(2)}) copy-start(s32[160]{0:T(256)} %copy-done.1) | copy-start | bytes 1924
  167.8 199.7 %reduce-scatter.2.cloned.1.call-start = ((), (), s32[]{:S(2)}) async-start(), calls=%async_computation.3 | async-start | bytes 4423680 | tf_op jit(solution)/shard_map/reduce_scatter | solution.py:84
  240.7 6.7 %copy-start.12 = (s32[4]{0:T(128)S(1)}, s32[4]{0:T(128)}, u32[]{:S(2)}) copy-start(s32[4]{0:T(128)} %copy-done.11) | copy-start | bytes 52
  252.3 8.1 %copy-start = (bf16[1,20,80,320]{3,2,1,0:T(8,128)(2,1)S(1)}, bf16[1,20,80,320]{3,2,1,0:T(8,128)(2,1)}, u32[]{:S(2)}) copy-start(bf16[1,20,80,320]{3,2,1,0:T(8,128)(2,1)} %get-tuple-element.8) | copy-start | bytes 3072004
  252.3 8.1 %copy-start.13 = (bf16[32,80,1600]{2,1,0:T(8,128)(2,1)S(1)}, bf16[32,80,1600]{2,1,0:T(8,128)(2,1)}, u32[]{:S(2)}) copy-start(bf16[32,80,1600]{2,1,0:T(8,128)(2,1)} %all-gather.3.cloned.1.call-done) | copy-start | bytes 24576004
Sparse Core Ops, SparseCore 0:
  168.0 56.5 all-gather.2
  285.2 82.2 reduce-scatter.1
where the time goes:
time: 387 us; the launch traced here: 381 us
  waiting for transfers between devices  117 us (30%)
  other arithmetic  98.3 us (25%)
  local copies, waits for them, and re-layouts  60.8 us (16%)
  blocking collectives  55.9 us (14%)
  matrix products  30.5 us (8%)
  between operations  14 us (4%)
  starting transfers between devices  4.31 us (1%)
    reduce_scatter x1, waiting for transfers between devices, body(): own = lax.psum_scatter(flat, 'fold', scatter_dimension=0, tiled=True)  82.2 us
    add x1, other arithmetic, body(): packed_w = packed_w + jnp.where(keep, cycle_block[..., cut], 0)  56.1 us
    all_to_all x1, blocking collectives, body(): lax.all_to_all(packed_k, 'fold', split_axis=0, concat_axis=0, tiled=True)  55.9 us
    all_to_all x1, waiting for transfers between devices, body(): lax.all_to_all(packed_c.reshape(n_i, k_local, n_pair, a_sub, v_pack), 'pa...  34.4 us
    dot_general x4, matrix products, body(): jnp.einsum('pfrx,xn->fprn', lhs, packed_w[s], preferred_element_type=jnp....  30.5 us
    reshape x2, local copies, waits for them, and re-layouts, body(): packed_w.reshape(c_local, FOLDS, k_pack, j_local * v_pack)  21.9 us
    add x1, other arithmetic, body(): total = total + jnp.where(keep, moved[:, s], 0)  16.6 us
    squeeze x4, local copies, waits for them, and re-layouts, body(): total = total + jnp.where(keep, moved[:, s], 0)  10.5 us
  transfers between devices with their start and end apart: 3, of which 2 were waited for; matrix products, arithmetic and copies ran while one was open for 23% of the time, Pallas kernels for 0%

commit v1 on v0

--- a/solution.py
+++ b/solution.py
@@ -59,7 +59,19 @@
     packed_k = jnp.concatenate(pieces, axis=-1)
     packed_k = packed_k.reshape(n_i, k_pack, a_sub, n_fold, c_local).transpose(3, 0, 2, 1, 4)
     packed_k = packed_k.reshape(n_fold, n_i * a_sub, k_pack * c_local)
-    relaid = lax.all_to_all(packed_k, "fold", split_axis=0, concat_axis=0, tiled=True)
+    opened, piece_out = (lax.axis_size("fold"), lax.axis_index("fold"))
+    arr_next = packed_k.shape[0] // opened
+    v1 = jnp.roll(packed_k, -piece_out * arr_next, axis=0)
+    rack = [lax.slice_in_dim(v1, 0, arr_next, axis=0)]
+    no = 1
+    while no < opened:
+        long_array = lax.slice_in_dim(v1, no * arr_next, (no + 1) * arr_next, axis=0)
+        rack.append(
+            lax.ppermute(long_array, "fold", [(b, (b + no) % opened) for b in range(opened)])
+        )
+        no = no + 1
+    arr_out = jnp.concatenate(rack[::-1], axis=0)
+    relaid = jnp.roll(arr_out, (piece_out + 1) * rack[0].shape[0], 0)
     gathered = lax.all_gather(relaid, "pair", axis=0, tiled=False)
     ckj = c_labels[:, None, None] ^ occ_labels[None, :, None] ^ j_labels[None, None, :]
     packed_w = 0

time: 387 us -> 389 us (level)
  blocking collectives: 55.9 us -> 0 us
  waiting for transfers between devices: 117 us -> 158 us
  starting transfers between devices: 4.31 us -> 13.1 us
  other arithmetic: 98.3 us -> 103 us
    all_to_all x1 -> x0, blocking collectives: 55.9 us -> none  [body(): lax.all_to_all(packed_k, 'fold', split_axis=0, concat_axis=0, tiled=True)]
    ppermute x0 -> x7, waiting for transfers between devices: none -> 40.1 us  [body(): lax.ppermute(long_array, 'fold', [(b, (b + no) % opened) for b in range(o...]
    ppermute x0 -> x7, starting transfers between devices: none -> 8.77 us  [body(): lax.ppermute(long_array, 'fold', [(b, (b + no) % opened) for b in range(o...]
    concatenate x0 -> x2, other arithmetic: none -> 4.75 us  [the longest x1 2.49 us: body(): v1 = jnp.roll(packed_k, -piece_out * arr_next, axis=0)]
  transfers between devices with their start and end apart: 3 -> 10, of which waited for: 2 -> 7; matrix products, arithmetic and copies ran while one was open for 23% -> 24% of each run, Pallas kernels for 0% -> 0%
where the time goes in v1:
time: 389 us; the launch traced here: 383 us
  waiting for transfers between devices  158 us (41%)
  other arithmetic  103 us (26%)
  local copies, waits for them, and re-layouts  63.2 us (16%)
  matrix products  30.6 us (8%)
  between operations  14.3 us (4%)
  starting transfers between devices  13.1 us (3%)
    reduce_scatter x1, waiting for transfers between devices, body(): own = lax.psum_scatter(flat, 'fold', scatter_dimension=0, tiled=True)  84 us
    add x1, other arithmetic, body(): packed_w = packed_w + jnp.where(keep, cycle_block[..., cut], 0)  56.3 us
    ppermute x7, waiting for transfers between devices, body(): lax.ppermute(long_array, 'fold', [(b, (b + no) % opened) for b in range(o...  40.1 us
    all_to_all x1, waiting for transfers between devices, body(): lax.all_to_all(packed_c.reshape(n_i, k_local, n_pair, a_sub, v_pack), 'pa...  34.2 us
    dot_general x4, matrix products, body(): jnp.einsum('pfrx,xn->fprn', lhs, packed_w[s], preferred_element_type=jnp....  30.6 us
    reshape x2, local copies, waits for them, and re-layouts, body(): packed_w.reshape(c_local, FOLDS, k_pack, j_local * v_pack)  21.9 us
    add x1, other arithmetic, body(): total = total + jnp.where(keep, moved[:, s], 0)  16.6 us
    add x1, other arithmetic, body(): packed_c = packed_c + jnp.where(keep, amplitudes[..., cut], 0)  9.53 us
  transfers between devices with their start and end apart: 10, of which 7 were waited for; matrix products, arithmetic and copies ran while one was open for 24% of the time, Pallas kernels for 0%

profile of v1, /device:TPU:0, one launch (start us, length us, event | category | flops | bytes accessed | tf_op | source)
XLA Modules:
  0.0 382.8 jit_solution(705772280742949971)
XLA Ops:
  10.3 9.5 %fusion.21 = bf16[4,20,80,160]{3,2,1,0:T(8,128)(2,1)S(1)} fusion(bf16[4,20,80,640]{3,2,1,0:T(8,128)(2,1)} %param.8, s32[160]{0:T(256)S(1)} %get-tuple-element.30, s32[160]{0:T(256)S(1)} %get-tuple-element.31, s32[160]{0:T(256)S(1)} %get-tuple-element.32, s32[160]{0:T(256)S(1)} %get-tuple-element.29, s32[4,20,80]{2,1,0:T(8,128)S(1)} %broadcast_xor_fusion.6), kind=kLoop, calls=%fused_computation.39 | loop fusion | flops 11264000 | bytes 10268160 | tf_op jit(solution)/shard_map/add | solution.py:41
  19.8 2.5 copy.45
  22.3 2.9 copy.46
  25.2 4.3 %all-to-all-start = ((bf16[4,20,4,20,160]{4,0,3,1,2:T(4,128)(2,1)}), bf16[4,20,4,20,160]{4,0,3,1,2:T(4,128)(2,1)S(1)}, u32[]{:S(2)}, u32[]{:S(2)}) async-start(bf16[4,20,4,20,160]{4,0,3,1,2:T(4,128)(2,1)} %copy.46), calls=%async_computation | async-start | bytes 6553600 | tf_op jit(solution)/shard_map/all_to_all | solution.py:42
  33.7 34.2 %all-to-all-done = bf16[4,20,4,20,160]{4,0,3,1,2:T(4,128)(2,1)S(1)} async-done(((bf16[4,20,4,20,160]{4,0,3,1,2:T(4,128)(2,1)}), bf16[4,20,4,20,160]{4,0,3,1,2:T(4,128)(2,1)S(1)}, u32[]{:S(2)}, u32[]{:S(2)}) %all-to-all-start) | async-done | bytes 2048032 | tf_op jit(solution)/shard_map/all_to_all | solution.py:42
  67.9 2.6 fusion.42
  70.5 3.0 squeeze.17
  73.5 2.5 squeeze.18
  76.6 2.5 squeeze.40
  79.1 16.6 %fusion.26 = (bf16[4,20,20,2,80]{4,3,0,2,1:T(2,128)(2,1)S(1)}, bf16[4,20,20,2,80]{4,3,0,2,1:T(2,128)(2,1)S(1)}, bf16[4,20,20,2,80]{4,3,0,2,1:T(2,128)(2,1)S(1)}, bf16[4,20,20,2,80]{4,3,0,2,1:T(2,128)(2,1)S(1)}) fusion(bf16[4,20,20,2,80]{4,3,0,2,1:T(2,128)(2,1)S(1)} %squeeze.40, s32[4,20,2,80]{3,2,0,1:T(2,128)S(1)} %get-tuple-element.25, ...), kind=kLoop, calls=%fused_computation.63 | loop fusion | flops 11264000 | bytes 4301120 | tf_op jit(solution)/shard_map/add | solution.py:57
  95.7 4.9 %maximum_bitcast_fusion = bf16[8,4,20,20,80]{4,0,1,2,3:T(8,128)(2,1)S(1)} fusion(bf16[4,20,20,2,80]{4,3,0,2,1:T(2,128)(2,1)S(1)} %get-tuple-element.11, bf16[4,20,20,2,80]{4,3,0,2,1:T(2,128)(2,1)S(1)} %get-tuple-element.12, bf16[4,20,20,2,80]{4,3,0,2,1:T(2,128)(2,1)S(1)} %get-tuple-element.13, bf16[4,20,20,2,80]{4,3,0,2,1:T(2,128)(2,1)S(1)} %get-tuple-element.10), kind=kLoop, calls=%fused_computation.40 | loop fusion | flops 8192000 | bytes 4096000 | tf_op jit(solution)/shard_map/transpose | solution.py:60
  100.6 4.1 %copy.47 = bf16[8,4,20,20,80]{4,3,2,1,0:T(8,128)(2,1)} copy(bf16[8,4,20,20,80]{4,0,1,2,3:T(8,128)(2,1)S(1)} %maximum_bitcast_fusion) | data formatting | bytes 4096000 | tf_op jit(solution)/shard_map/transpose | solution.py:60
  104.7 6.3 %reshape.385 = bf16[8,80,1600]{2,1,0:T(8,128)(2,1)} reshape(bf16[8,4,20,20,80]{4,3,2,1,0:T(8,128)(2,1)} %copy.47) | data formatting | bytes 4096000 | tf_op jit(solution)/shard_map/reshape | solution.py:61
  111.0 2.5 fusion.23
  114.4 5.3 %collective-permute-start = (bf16[1,80,1600]{2,1,0:T(8,128)(2,1)}, bf16[1,80,1600]{2,1,0:T(8,128)(2,1)}, u32[]{:S(2)}, u32[]{:S(2)}) collective-permute-start(bf16[1,80,1600]{2,1,0:T(8,128)(2,1)} %get-tuple-element.24), channel_id=1, source_target_pairs={{0,7},{1,0},{2,1},{3,2},{4,3},{5,4},{6,5},{7,6},{8,15},{9,8},{10,9... | collective-permute-start | bytes 768008 | tf_op jit(solution)/shard_map/ppermute | solution.py:70
  120.1 3.0 collective-permute-start.3
  123.1 3.7 collective-permute-done
  127.9 4.7 %collective-permute-done.1 = bf16[1,80,1600]{2,1,0:T(8,128)(2,1)} collective-permute-done((bf16[1,80,1600]{2,1,0:T(8,128)(2,1)}, bf16[1,80,1600]{2,1,0:T(8,128)(2,1)}, u32[]{:S(2)}, u32[]{:S(2)}) %collective-permute-start.1) | collective-permute-done | bytes 256032 | tf_op jit(solution)/shard_map/ppermute | solution.py:70
  133.6 4.7 %collective-permute-done.2 = bf16[1,80,1600]{2,1,0:T(8,128)(2,1)S(1)} collective-permute-done((bf16[1,80,1600]{2,1,0:T(8,128)(2,1)S(1)}, bf16[1,80,1600]{2,1,0:T(8,128)(2,1)S(1)}, u32[]{:S(2)}, u32[]{:S(2)}) %collective-permute-start.2) | collective-permute-done | bytes 256032 | tf_op jit(solution)/shard_map/ppermute | solution.py:70
  138.3 26.8 %collective-permute-done.3 = bf16[1,80,1600]{2,1,0:T(8,128)(2,1)S(1)} collective-permute-done((bf16[1,80,1600]{2,1,0:T(8,128)(2,1)S(1)}, bf16[1,80,1600]{2,1,0:T(8,128)(2,1)S(1)}, u32[]{:S(2)}, u32[]{:S(2)}) %collective-permute-start.3) | collective-permute-done | bytes 256032 | tf_op jit(solution)/shard_map/ppermute | solution.py:70
  165.5 2.3 fusion.22
  169.4 56.3 %fusion.14 = bf16[80,80,2,160]{3,2,1,0:T(2,128)(2,1)} fusion(bf16[80,80,2,640]{3,2,1,0:T(2,128)(2,1)} %param.9, s32[160]{0:T(256)S(1)} %get-tuple-element.30, s32[80,80,2]{2,1,0:T(8,128)S(1)} %broadcast_xor_fusion, s32[160]{0:T(256)S(1)} %get-tuple-element.31, s32[160]{0:T(256)S(1)} %copy-done.3, s32[160]{0:T(256)S(1)} %get-tuple-element.29), kind=kLoop, calls=%fused_computation.22 | loop fusion | flops 22528000 | bytes 20533760 | tf_op jit(solution)/shard_map/add | solution.py:81
  225.7 15.1 %reshape.394 = bf16[80,4,20,320]{3,2,1,0:T(8,128)(2,1)} reshape(bf16[80,80,2,160]{3,2,1,0:T(2,128)(2,1)} %fusion.14) | data formatting | bytes 8192000 | tf_op jit(solution)/shard_map/reshape | solution.py:82
  240.9 6.7 %copy.64 = bf16[80,4,20,320]{3,0,2,1:T(8,128)(2,1)} copy(bf16[80,4,20,320]{3,2,1,0:T(8,128)(2,1)} %reshape.394) | data formatting | bytes 8192000 | tf_op jit(solution)/shard_map/reshape | solution.py:82
  248.1 4.3 %fusion.41 = (bf16[1,20,80,320]{3,2,1,0:T(8,128)(2,1)S(1)}, bf16[1,20,80,320]{3,2,1,0:T(8,128)(2,1)S(1)}, bf16[1,20,80,320]{3,2,1,0:T(8,128)(2,1)}, bf16[1,20,80,320]{3,2,1,0:T(8,128)(2,1)}) fusion(bf16[4,20,80,320]{3,2,1,0:T(8,128)(2,1)} %bitcast.46), kind=kLoop, calls=%fused_computation.108 | loop fusion | bytes 8192000 | tf_op jit(solution)/shard_map/slice | solution.py:93
  252.5 8.2 %fusion.1 = f32[320,4,8,80]{0,3,2,1:T(8,128)S(1)} fusion(bf16[1600,320,1,1]{1,0,3,2:T(8,128)(2,1)} %bitcast.55, bf16[4,8,80,1600]{3,2,1,0:T(8,128)(2,1)} %bitcast.58, s32[1600]{0:T(1024)S(1)} %xor.329, s32[4,8,80]{2,1,0:T(8,128)S(1)} %broadcast_xor_fusion.8), kind=kOutput, calls=%fused_computation.9 | convolution fusion | flops 2629632000 | bytes 12509440 | tf_op jit(solution)/shard_map/pfrx,xn->fprn/dot_general | solution.py:92
  260.6 7.1 %fusion = f32[320,4,8,80]{0,3,2,1:T(8,128)} fusion(bf16[1600,320,1,1]{1,0,3,2:T(8,128)(2,1)S(1)} %bitcast.54, bf16[4,8,80,1600]{3,2,1,0:T(8,128)(2,1)S(1)} %bitcast.59, s32[1600]{0:T(1024)S(1)} %xor.306, s32[4,8,80]{2,1,0:T(8,128)S(1)} %broadcast_xor_fusion.8), kind=kOutput, calls=%fused_computation.8 | convolution fusion | flops 2629632000 | bytes 12509440 | tf_op jit(solution)/shard_map/pfrx,xn->fprn/dot_general | solution.py:92
  267.7 7.0 %fusion.2 = f32[320,4,8,80]{0,3,2,1:T(8,128)} fusion(bf16[1600,320,1,1]{1,0,3,2:T(8,128)(2,1)S(1)} %bitcast.53, bf16[4,8,80,1600]{3,2,1,0:T(8,128)(2,1)S(1)} %bitcast.60, s32[1600]{0:T(1024)S(1)} %xor.332, s32[4,8,80]{2,1,0:T(8,128)S(1)} %broadcast_xor_fusion.8), kind=kOutput, calls=%fused_computation.10 | convolution fusion | flops 2629632000 | bytes 12509440 | tf_op jit(solution)/shard_map/pfrx,xn->fprn/dot_general | solution.py:92
  274.8 8.3 %add_bitcast_fusion = f32[8,4,80,320]{3,2,0,1:T(8,128)S(1)} fusion(f32[320,4,8,80]{0,3,2,1:T(8,128)} %fusion.2, f32[320,4,8,80]{0,3,2,1:T(8,128)} %fusion, f32[320,4,8,80]{0,3,2,1:T(8,128)S(1)} %fusion.1, bf16[1600,320,1,1]{1,0,3,2:T(8,128)(2,1)S(1)} %bitcast.52, bf16[4,8,80,1600]{3,2,1,0:T(8,128)(2,1)S(1)} %bitcast.61, s32[1600]{0:T(1024)S(1)} %xor.335, ...), kind=kOutput, calls=%fused_computation.36 | convolution fusion | flops 2632089600 | bytes 22339840 | tf_op jit(solution)/shard_map/pfrx,xn->fprn/dot_general | solution.py:92
  283.1 2.2 copy.52
  285.5 84.0 %reduce-scatter.2.cloned.1.call-done = f32[320,320]{1,0:T(8,128)} async-done(((f32[2560,320]{1,0:T(8,128)}), f32[320,320]{1,0:T(8,128)}) %reduce-scatter.2.cloned.1.call-update) | async-done | bytes 409616 | tf_op jit(solution)/shard_map/reduce_scatter | solution.py:96
  371.0 4.5 %compare_select_fusion.32 = bf16[4,80,2,640]{3,2,1,0:T(2,128)(2,1)} fusion(bf16[4,80,2,160]{3,2,1,0:T(2,128)(2,1)S(1)} %bitcast.50, s32[640]{0:T(1024)S(1)} %convert_reduce_fusion, s32[4,80,2]{2,1,0:T(8,128)S(1)} %broadcast_xor_fusion.1), kind=kLoop, calls=%fused_computation.57 | loop fusion | flops 4096000 | bytes 1029120 | tf_op jit(solution)/shard_map/jit(_where)/select_n | solution.py:101
  (93 shorter events, 15.9 us)
Async XLA Ops:
  7.5 22.6 %copy-start.2 = (s32[160]{0:T(256)}, s32[160]{0:T(256)S(1)}, u32[]{:S(2)}) copy-start(s32[160]{0:T(256)S(1)} %get-tuple-element.32) | copy-start | bytes 1924
  7.6 12.2 %copy-start.4 = (s32[80]{0:T(128)}, s32[80]{0:T(128)S(1)}, u32[]{:S(2)}) copy-start(s32[80]{0:T(128)S(1)} %dynamic_slice.18) | copy-start | bytes 964
  10.1 9.7 %copy-start.12 = (s32[4]{0:T(128)}, s32[4]{0:T(128)S(1)}, u32[]{:S(2)}) copy-start(s32[4]{0:T(128)S(1)} %select_reduce_fusion) | copy-start | bytes 52
  25.2 42.7 %all-to-all-start = ((bf16[4,20,4,20,160]{4,0,3,1,2:T(4,128)(2,1)}), bf16[4,20,4,20,160]{4,0,3,1,2:T(4,128)(2,1)S(1)}, u32[]{:S(2)}, u32[]{:S(2)}) async-start(bf16[4,20,4,20,160]{4,0,3,1,2:T(4,128)(2,1)} %copy.46), calls=%async_computation | async-start | bytes 6553600 | tf_op jit(solution)/shard_map/all_to_all | solution.py:42
  29.5 223.0 %all-gather.3.cloned.1.call-start = ((), (), s32[]{:S(2)}) async-start(), calls=%async_computation.3 | async-start | bytes 10649600 | tf_op jit(solution)/shard_map/all_gather | solution.py:75
  70.5 5.5 %copy-start = (bf16[4,1,20,20,160]{4,0,3,2,1:T(4,128)(2,1)S(1)}, bf16[4,1,20,20,160]{4,0,3,2,1:T(4,128)(2,1)}, u32[]{:S(2)}) copy-start(bf16[4,1,20,20,160]{4,0,3,2,1:T(4,128)(2,1)} %get-tuple-element.16) | copy-start | bytes 1536004
  70.5 8.6 %copy-start.6 = (s32[20]{0:T(128)S(1)}, s32[20]{0:T(128)}, u32[]{:S(2)}) copy-start(s32[20]{0:T(128)} %get-tuple-element.37) | copy-start | bytes 244
  70.5 8.7 %copy-start.7 = (s32[20]{0:T(128)S(1)}, s32[20]{0:T(128)}, u32[]{:S(2)}) copy-start(s32[20]{0:T(128)} %get-tuple-element.38) | copy-start | bytes 244
  70.5 8.7 %copy-start.9 = (s32[20]{0:T(128)S(1)}, s32[20]{0:T(128)}, u32[]{:S(2)}) copy-start(s32[20]{0:T(128)} %get-tuple-element.39) | copy-start | bytes 244
  114.4 12.5 %collective-permute-start = (bf16[1,80,1600]{2,1,0:T(8,128)(2,1)}, bf16[1,80,1600]{2,1,0:T(8,128)(2,1)}, u32[]{:S(2)}, u32[]{:S(2)}) collective-permute-start(bf16[1,80,1600]{2,1,0:T(8,128)(2,1)} %get-tuple-element.24), channel_id=1, source_target_pairs={{0,7},{1,0},{2,1},{3,2},{4,3},{5,4},{6,5},{7,6},{8,15},{9,8},{10,9... | collective-permute-start | bytes 768008 | tf_op jit(solution)/shard_map/ppermute | solution.py:70
  119.7 12.9 %collective-permute-start.1 = (bf16[1,80,1600]{2,1,0:T(8,128)(2,1)}, bf16[1,80,1600]{2,1,0:T(8,128)(2,1)}, u32[]{:S(2)}, u32[]{:S(2)}) collective-permute-start(bf16[1,80,1600]{2,1,0:T(8,128)(2,1)} %get-tuple-element.23), channel_id=1, source_target_pairs={{0,6},{1,7},{2,0},{3,1},{4,2},{5,3},{6,4},{7,5},{8,14},{9,15},{10,... | collective-permute-start | bytes 768008 | tf_op jit(solution)/shard_map/ppermute | solution.py:70
  120.1 18.1 %collective-permute-start.2 = (bf16[1,80,1600]{2,1,0:T(8,128)(2,1)S(1)}, bf16[1,80,1600]{2,1,0:T(8,128)(2,1)S(1)}, u32[]{:S(2)}, u32[]{:S(2)}) collective-permute-start(bf16[1,80,1600]{2,1,0:T(8,128)(2,1)S(1)} %get-tuple-element.22), channel_id=1, source_target_pairs={{0,5},{1,6},{2,7},{3,0},{4,1},{5,2},{6,3},{7,4},{8,13},{9,14},{10,... | collective-permute-start | bytes 768008 | tf_op jit(solution)/shard_map/ppermute | solution.py:70
  120.1 44.9 %collective-permute-start.3 = (bf16[1,80,1600]{2,1,0:T(8,128)(2,1)S(1)}, bf16[1,80,1600]{2,1,0:T(8,128)(2,1)S(1)}, u32[]{:S(2)}, u32[]{:S(2)}) collective-permute-start(bf16[1,80,1600]{2,1,0:T(8,128)(2,1)S(1)} %get-tuple-element.21), channel_id=1, source_target_pairs={{0,4},{1,5},{2,6},{3,7},{4,0},{5,1},{6,2},{7,3},{8,12},{9,13},{10,... | collective-permute-start | bytes 768008 | tf_op jit(solution)/shard_map/ppermute | solution.py:70
  123.1 42.1 %collective-permute-start.4 = (bf16[1,80,1600]{2,1,0:T(8,128)(2,1)S(1)}, bf16[1,80,1600]{2,1,0:T(8,128)(2,1)S(1)}, u32[]{:S(2)}, u32[]{:S(2)}) collective-permute-start(bf16[1,80,1600]{2,1,0:T(8,128)(2,1)S(1)} %get-tuple-element.20), channel_id=1, source_target_pairs={{0,3},{1,4},{2,5},{3,6},{4,7},{5,0},{6,1},{7,2},{8,11},{9,12},{10,... | collective-permute-start | bytes 768008 | tf_op jit(solution)/shard_map/ppermute | solution.py:70
  126.9 38.4 %collective-permute-start.5 = (bf16[1,80,1600]{2,1,0:T(8,128)(2,1)S(1)}, bf16[1,80,1600]{2,1,0:T(8,128)(2,1)S(1)}, u32[]{:S(2)}, u32[]{:S(2)}) collective-permute-start(bf16[1,80,1600]{2,1,0:T(8,128)(2,1)S(1)} %get-tuple-element.19), channel_id=1, source_target_pairs={{0,2},{1,3},{2,4},{3,5},{4,6},{5,7},{6,0},{7,1},{8,10},{9,11},{10,... | collective-permute-start | bytes 768008 | tf_op jit(solution)/shard_map/ppermute | solution.py:70
  132.6 32.8 %collective-permute-start.6 = (bf16[1,80,1600]{2,1,0:T(8,128)(2,1)S(1)}, bf16[1,80,1600]{2,1,0:T(8,128)(2,1)S(1)}, u32[]{:S(2)}, u32[]{:S(2)}) collective-permute-start(bf16[1,80,1600]{2,1,0:T(8,128)(2,1)S(1)} %get-tuple-element.18), channel_id=1, source_target_pairs={{0,1},{1,2},{2,3},{3,4},{4,5},{5,6},{6,7},{7,0},{8,9},{9,10},{10,1... | collective-permute-start | bytes 768008 | tf_op jit(solution)/shard_map/ppermute | solution.py:70
  165.4 2.5 copy-start.5
  165.4 2.5 copy-start.8
  165.4 2.5 copy-start.10
  165.4 2.5 copy-start.11
  165.5 2.7 copy-start.15
  167.7 1.7 copy-start.3
  167.8 201.8 %reduce-scatter.2.cloned.1.call-start = ((), (), s32[]{:S(2)}) async-start(), calls=%async_computation.2 | async-start | bytes 4423680 | tf_op jit(solution)/shard_map/reduce_scatter | solution.py:96
  240.9 6.7 %copy-start.13 = (s32[4]{0:T(128)S(1)}, s32[4]{0:T(128)}, u32[]{:S(2)}) copy-start(s32[4]{0:T(128)} %copy-done.12) | copy-start | bytes 52
  252.4 8.2 %copy-start.1 = (bf16[1,20,80,320]{3,2,1,0:T(8,128)(2,1)S(1)}, bf16[1,20,80,320]{3,2,1,0:T(8,128)(2,1)}, u32[]{:S(2)}) copy-start(bf16[1,20,80,320]{3,2,1,0:T(8,128)(2,1)} %get-tuple-element.9) | copy-start | bytes 3072004
  252.5 8.2 %copy-start.14 = (bf16[32,80,1600]{2,1,0:T(8,128)(2,1)S(1)}, bf16[32,80,1600]{2,1,0:T(8,128)(2,1)}, u32[]{:S(2)}) copy-start(bf16[32,80,1600]{2,1,0:T(8,128)(2,1)} %all-gather.3.cloned.1.call-done) | copy-start | bytes 24576004
Sparse Core Ops, SparseCore 0:
  167.9 58.4 all-gather.2
  285.4 84.0 reduce-scatter.1
